TPU v7x, 256 devices: a whole 4x4x8 slice. The times are simulated.
256 devices in a mesh: dp: 8 (over x, core), ctx: 32 (over y, z).
Axes of the slice: x: 4, y: 4, z: 8, core: 2. Of those that a mesh axis runs over, the one named last changes fastest.
Arguments:
- tokens: bfloat16 [32768, 4096], P(('dp', 'ctx')), parts along dimension 0, may hold values from -6 to 6
- pick_flags: int32 [32768], P(('dp', 'ctx')), parts along dimension 0, may hold values from 0 to 1, as said below
- gate_scales: bfloat16 [32768], P(('dp', 'ctx')), parts along dimension 0, may hold values from 0.099609375 to 1
- attn_gain: float32 [4096], replicated, may hold values from 0.4 to 1.6
- query_weight: bfloat16 [4096, 4096], P(None, 'ctx')
- key_weight: bfloat16 [4096, 1024], P(None, 'ctx')
- value_matrix: bfloat16 [4096, 1024], P(None, 'ctx'), may hold values from -0.09375 to 0.09375
- output_weight: bfloat16 [4096, 4096], P('ctx'), may hold values from -0.09375 to 0.09375
- ffn_gain: float32 [4096], replicated, may hold values from 0.25 to 1.75
- gate_weight: bfloat16 [4096, 11264], P(None, 'ctx'), may hold values from -0.09375 to 0.09375
- up_weight: bfloat16 [4096, 11264], P(None, 'ctx'), may hold values from -0.09375 to 0.09375
- down_weight: bfloat16 [11264, 4096], P('ctx'), may hold values from -0.0546875 to 0.0546875
Outputs:
- block_out: bfloat16 [32768, 4096], P(('dp', 'ctx')), parts along dimension 0
There are 8 independent parts, one for each index of `dp`. A program takes and returns all parts, laid end to end along the dimension named above; an argument that names none is the same for every part. Nothing has to cross between parts.
Inputs may be any that keep to these rules, and one draw needn't show every extreme that they name: `pick_flags`: each device's 128 tokens hold at most 32 picks, the first device exactly 32; each document holds exactly 512 picks; a device may hold none.
All inputs are finite; a program needn't handle non-finite values.
Results may differ from a plain program's by a relative error of at most 0.01.
Values may be sent and summed in bfloat16 or wider, within the bound.
A program may use at most 128 MiB of HBM per device.

v0:
```python
import jax
import jax.numpy as jnp
from jax import lax
from jax.sharding import Mesh, PartitionSpec as P

QUERY_HEADS = 32
KEY_VALUE_HEADS = 8
HEAD_SIZE = 128
PICK_DEV = 16
MOST = 32
Z_RUN = 8
GROUP = ("cy", "cz")
norm_eps = 1e-05
rope_base = 500000.0


def rms_scale(matrix, gain_vec):
    mean_square = jnp.mean(matrix * matrix, axis=-1, keepdims=True)
    return matrix * lax.rsqrt(mean_square + norm_eps) * gain_vec


def apply_rotary(values, token_positions):
    half_dim = values.shape[-1] // 2
    frequency = rope_base ** (-(jnp.arange(half_dim, dtype=jnp.float32) * 2.0) / values.shape[-1])
    angles = token_positions.astype(jnp.float32)[:, None] * frequency[None, :]
    cosine = jnp.cos(angles)
    sine_part = jnp.sin(angles)
    lower_half = values[..., :half_dim]
    upper_half = values[..., half_dim:]
    return jnp.concatenate(
        (
            lower_half * cosine - upper_half * sine_part,
            upper_half * cosine + lower_half * sine_part,
        ),
        axis=-1,
    )


def reduce_scatter_rows(partial, y_size, z_size):
    rows, width = partial.shape
    blocks = partial.reshape(z_size, y_size, rows // (y_size * z_size), width)
    over_y = lax.all_to_all(blocks, "cy", 1, 1, tiled=True)
    part = jnp.sum(over_y.astype(jnp.float32), axis=1).astype(jnp.bfloat16)
    over_z = lax.all_to_all(part, "cz", 0, 0, tiled=True)
    return jnp.sum(over_z.astype(jnp.float32), axis=0)


def gather_rows(x):
    return lax.all_gather(lax.all_gather(x, "cy", axis=0, tiled=True), "cz", axis=0, tiled=True)


def body(
    tokens,
    pick_flags,
    gate_scales,
    attn_gain,
    query_weight,
    key_weight,
    value_matrix,
    output_weight,
    ffn_gain,
    gate_weight,
    up_weight,
    down_weight,
):
    tok_local, width = tokens.shape
    y_size = lax.axis_size("cy")
    z_size = lax.axis_size("cz")
    ctx_size = y_size * z_size
    my_index = lax.axis_index("cy") * z_size + lax.axis_index("cz")
    blk = jnp.arange(ctx_size, dtype=jnp.int32)
    block_dev = blk % y_size * z_size + blk // y_size
    picked_count = PICK_DEV * ctx_size
    slots = MOST * ctx_size
    half_pick = PICK_DEV // 2
    half_cycle = ctx_size // 2
    slot_of = jnp.cumsum(pick_flags) - 1
    token_ids = jnp.arange(tok_local, dtype=jnp.int32)
    slot_match = (jnp.arange(MOST, dtype=jnp.int32)[:, None] == slot_of[None, :]) & (
        pick_flags[None, :] == 1
    )
    chosen = jnp.sum(jnp.where(slot_match, token_ids[None, :], 0), axis=1)
    filled = jnp.any(slot_match, axis=1)
    local_index = jnp.where(filled, chosen, -1)
    padded_rows = jnp.where(filled[:, None], tokens[chosen], jnp.zeros((), jnp.bfloat16))
    padded_gate = jnp.where(filled, gate_scales[chosen], jnp.zeros((), jnp.bfloat16))
    lane = jnp.arange(128, dtype=jnp.int32)[None, :]
    extra = jnp.where(
        lane == 0,
        local_index.astype(jnp.bfloat16)[:, None],
        jnp.where(lane == 1, padded_gate[:, None], jnp.zeros((), jnp.bfloat16)),
    )
    packed = jnp.concatenate((padded_rows, extra), axis=1)
    all_packed = gather_rows(packed)
    all_index = all_packed[:, width].astype(jnp.int32)
    slot_filled = all_index >= 0
    counts_blk = jnp.sum(slot_filled.reshape(ctx_size, MOST).astype(jnp.int32), axis=1)
    counts = counts_blk.reshape(z_size, y_size).T.reshape(ctx_size)
    run_ends = jnp.cumsum(counts)
    run_starts = run_ends - counts
    slot_ids = jnp.arange(slots, dtype=jnp.int32)
    slot_pos = block_dev[slot_ids // MOST] * tok_local + all_index
    rope_pos = jnp.where(slot_filled, slot_pos, 0)
    never = jnp.int32(1 << 30)
    mask_pos = jnp.where(slot_filled, slot_pos, never)
    normalized = rms_scale(all_packed[:, :width].astype(jnp.float32), attn_gain).astype(
        jnp.bfloat16
    )
    queries = jnp.dot(normalized, query_weight, preferred_element_type=jnp.float32)
    queries = apply_rotary(queries, rope_pos).astype(jnp.bfloat16)
    kv_weight = jnp.concatenate((key_weight, value_matrix), axis=1)
    kv_local = jnp.einsum(
        "pd,dc->cp", normalized, kv_weight, preferred_element_type=jnp.float32
    ).astype(jnp.bfloat16)
    comps = key_weight.shape[1] // KEY_VALUE_HEADS
    query_group_width = QUERY_HEADS // KEY_VALUE_HEADS
    by_head = jnp.transpose(kv_local.reshape(2, comps, KEY_VALUE_HEADS, slots), (2, 0, 1, 3))
    send = jnp.repeat(by_head, query_group_width, axis=0)
    got = lax.all_to_all(send, GROUP, 0, 0, tiled=True)
    key_cols = got[:, 0].reshape(ctx_size * comps, slots)
    value_cols = got[:, 1].reshape(ctx_size * comps, slots)
    keys_here = apply_rotary(key_cols.T.astype(jnp.float32), rope_pos).astype(jnp.bfloat16)
    values_here = value_cols.T
    scores = jnp.dot(queries, keys_here.T, preferred_element_type=jnp.float32) / jnp.sqrt(
        jnp.float32(HEAD_SIZE)
    )
    allowed = mask_pos[None, :] <= mask_pos[:, None]
    scores = jnp.where(allowed, scores, -jnp.inf)
    row_max = jnp.max(scores, axis=1, keepdims=True)
    exp_terms = jnp.exp(scores - row_max)
    prob_bf = (exp_terms / jnp.sum(exp_terms, axis=1, keepdims=True)).astype(jnp.bfloat16)
    head_pad = jnp.dot(prob_bf, values_here, preferred_element_type=jnp.float32).astype(
        jnp.bfloat16
    )
    order_ids = jnp.arange(picked_count, dtype=jnp.int32)
    owner_of = order_ids // PICK_DEV
    within = order_ids % PICK_DEV
    low_part = within < half_pick
    rank_block = jnp.where(low_part, owner_of, (owner_of + half_cycle) % ctx_size)
    rank_inner = jnp.where(low_part, 2 * within, 2 * (within - half_pick) + 1)
    rank_ids = rank_block * PICK_DEV + rank_inner
    before = (run_ends[None, :] <= rank_ids[:, None]).astype(jnp.int32)
    source = jnp.sum(before, axis=1)
    offset = rank_ids - jnp.sum(before * counts[None, :], axis=1)
    flat_row = (source % z_size * y_size + source // z_size) * MOST + offset
    flat_blocked = flat_row.reshape(ctx_size, PICK_DEV)[block_dev].reshape(picked_count)
    pick_onehot = (flat_blocked[:, None] == slot_ids[None, :]).astype(jnp.bfloat16)
    head_out = jnp.dot(pick_onehot, head_pad, preferred_element_type=jnp.float32).astype(
        jnp.bfloat16
    )
    own_start = my_index * PICK_DEV
    own_flat = lax.dynamic_slice_in_dim(flat_row, own_start, PICK_DEV, 0)
    own_packed = all_packed[own_flat]
    own_rows = own_packed[:, :width].astype(jnp.float32)
    scale_own = own_packed[:, width + 1].astype(jnp.float32)
    attn_own = reduce_scatter_rows(
        jnp.dot(head_out, output_weight, preferred_element_type=jnp.float32).astype(jnp.bfloat16),
        y_size,
        z_size,
    )
    mixed_own = own_rows + attn_own
    normed_own = rms_scale(mixed_own, ffn_gain).astype(jnp.bfloat16)
    normed_ffn = gather_rows(normed_own)
    gate_proj = jnp.dot(normed_ffn, gate_weight, preferred_element_type=jnp.float32)
    up_proj = jnp.dot(normed_ffn, up_weight, preferred_element_type=jnp.float32)
    hidden = (jax.nn.silu(gate_proj) * up_proj).astype(jnp.bfloat16)
    ffn_own = reduce_scatter_rows(
        jnp.dot(hidden, down_weight, preferred_element_type=jnp.float32).astype(jnp.bfloat16),
        y_size,
        z_size,
    )
    final_own = (own_rows + scale_own[:, None] * (attn_own + ffn_own)).astype(jnp.bfloat16)
    own_source = lax.dynamic_slice_in_dim(source, own_start, PICK_DEV, 0)
    targets = jnp.arange(ctx_size, dtype=jnp.int32)[:, None]
    first_half = (own_source[None, :half_pick] == targets)[:, :, None]
    second_half = (own_source[None, half_pick:] == targets)[:, :, None]
    zero = jnp.zeros((), jnp.bfloat16)
    back = jnp.where(
        first_half,
        final_own[None, :half_pick],
        jnp.where(second_half, final_own[None, half_pick:], zero),
    )
    returned = lax.all_to_all(back, GROUP, 0, 0, tiled=True).reshape(ctx_size * half_pick, width)
    my_start = run_starts[my_index]
    rank_here = jnp.clip(my_start + slot_of, 0, picked_count - 1)
    inner_here = rank_here % PICK_DEV
    odd_here = inner_here % 2
    owner_here = (rank_here // PICK_DEV + odd_here * half_cycle) % ctx_size
    take_rows = owner_here * half_pick + inner_here // 2
    return jnp.where(pick_flags[:, None] == 1, returned[take_rows], tokens)


def solution(mesh):
    dp_size, ctx_size = mesh.devices.shape
    z_size = Z_RUN if ctx_size % Z_RUN == 0 else ctx_size
    split = Mesh(mesh.devices.reshape(dp_size, ctx_size // z_size, z_size), ("dp", "cy", "cz"))
    rows = ("dp", "cy", "cz")
    in_specs = (
        P(rows, None),
        P(rows),
        P(rows),
        P(),
        P(None, GROUP),
        P(None, GROUP),
        P(None, GROUP),
        P(GROUP, None),
        P(),
        P(None, GROUP),
        P(None, GROUP),
        P(GROUP, None),
    )
    out_specs = P(rows, None)
    return jax.shard_map(body, mesh=split, in_specs=in_specs, out_specs=out_specs, check_vma=False)
```

profile of v0, /device:TPU:2, one launch (start us, length us, event | category | flops | bytes accessed | tf_op | source)
XLA Modules:
  0.0 529.0 jit_solution(11144931826340381880)
XLA Ops:
  13.4 29.7 %all-gather.4.cloned.1.call-done = bf16[128,4224]{1,0:T(8,128)(2,1)} async-done(((bf16[32,4224]{1,0:T(8,128)(2,1)}), bf16[128,4224]{1,0:T(8,128)(2,1)}) %all-gather.4.cloned.1.call-update) | async-done | bytes 1081360 | tf_op jit(solution)/shard_map/all_gather | solution.py:49
  48.6 4.6 select_reduce_fusion
  54.0 15.4 %select_multiply_fusion = s32[1024]{0:T(1024)S(1)} fusion(pred[1024]{0:T(1024)(128)(4,1)S(1)} %fusion.56, pred[1024]{0:T(1024)(128)(4,1)S(1)} %fusion.57, pred[1024]{0:T(1024)(128)(4,1)S(1)} %fusion.80, pred[1024]{0:T(1024)(128)(4,1)S(1)} %fusion.79, pred[1024]{0:T(1024)(128)(4,1)S(1)} %fusion.78, pred[1024]{0:T(1024)(128)(4,1)S(1)} %fusion.77, ...), kind=kLoop, calls=%fused_computation.217 | loop fusion | flops 26624 | bytes 33892 | tf_op jit(solution)/shard_map/mul | solution.py:102
  70.1 72.0 %all-gather.6.cloned.1.call-done = bf16[1024,4224]{1,0:T(8,128)(2,1)} async-done(((bf16[128,4224]{1,0:T(8,128)(2,1)}), bf16[1024,4224]{1,0:T(8,128)(2,1)}) %all-gather.6.cloned.1.call-update) | async-done | bytes 8650768 | tf_op jit(solution)/shard_map/all_gather | solution.py:49
  144.1 5.1 fusion
  149.3 5.2 fusion.13
  155.6 7.5 %all-to-all-start = ((bf16[32,2,4,1024]{3,2,1,0:T(4,128)(2,1)}), bf16[32,2,4,1024]{3,2,1,0:T(4,128)(2,1)}, u32[]{:S(2)}, u32[]{:S(2)}) async-start(bf16[32,2,4,1024]{3,2,1,0:T(4,128)(2,1)} %bitcast.61), calls=%async_computation | async-start | bytes 1048576 | tf_op jit(solution)/shard_map/all_to_all | solution.py:119
  165.4 7.2 %fusion.9 = f32[1024,128]{0,1:T(8,128)} fusion(bf16[4096,128]{1,0:T(8,128)(2,1)} %param.16, f32[4096]{0:T(1024)} %param.15, f32[1024]{0:T(1024)S(1)} %add_rsqrt_fusion, bf16[1024,4224]{1,0:T(8,128)(2,1)} %all-gather.6.cloned.1.call-done), kind=kOutput, calls=%fused_computation.25 | convolution fusion | flops 1090519040 | bytes 9981952 | tf_op jit(solution)/shard_map/dot_general | solution.py:109
  172.6 7.1 %all-to-all-done = bf16[32,2,4,1024]{3,2,1,0:T(4,128)(2,1)} async-done(((bf16[32,2,4,1024]{3,2,1,0:T(4,128)(2,1)}), bf16[32,2,4,1024]{3,2,1,0:T(4,128)(2,1)}, u32[]{:S(2)}, u32[]{:S(2)}) %all-to-all-start) | async-done | bytes 524320 | tf_op jit(solution)/shard_map/all_to_all | solution.py:119
  190.4 5.3 convolution_convert_fusion
  198.1 49.8 %all_to_all.30 = bf16[8,4,16,4096]{3,2,0,1:T(8,128)(2,1)} all-to-all(bf16[8,4,16,4096]{3,2,0,1:T(8,128)(2,1)S(1)} %copy.38), channel_id=1, replica_groups=mesh['dp'=8,'cy'=4,'cz'=8] {'cy'}, dimensions={1} | all-to-all | bytes 8388608 | tf_op jit(solution)/shard_map/all_to_all | solution.py:42
  252.1 5.7 %all-to-all-start.2 = ((bf16[8,16,4096]{2,1,0:T(8,128)(2,1)}), bf16[8,16,4096]{2,1,0:T(8,128)(2,1)}, u32[]{:S(2)}, u32[]{:S(2)}) async-start(bf16[8,16,4096]{2,1,0:T(8,128)(2,1)} %reduce_sum.120), calls=%async_computation.2 | async-start | bytes 2097152 | tf_op jit(solution)/shard_map/all_to_all | solution.py:44
  258.2 5.3 %gather_fusion.2 = bf16[16,4224]{1,0:T(8,128)(2,1)S(1)} fusion(bf16[1024,4224]{1,0:T(8,128)(2,1)} %all-gather.6.cloned.1.call-done, s32[1024]{0:T(1024)S(1)} %pad_clamp_fusion.2), kind=kCustom, calls=%fused_computation.2 | custom fusion | bytes 270400 | tf_op jit(solution)/shard_map/gather | solution.py:153
  263.5 21.2 %all-to-all-done.2 = bf16[8,16,4096]{2,1,0:T(8,128)(2,1)} async-done(((bf16[8,16,4096]{2,1,0:T(8,128)(2,1)}), bf16[8,16,4096]{2,1,0:T(8,128)(2,1)}, u32[]{:S(2)}, u32[]{:S(2)}) %all-to-all-start.2) | async-done | bytes 1048608 | tf_op jit(solution)/shard_map/all_to_all | solution.py:44
  286.4 13.5 %all_gather.14 = bf16[64,4096]{1,0:T(8,128)(2,1)} all-gather(bf16[16,4096]{1,0:T(8,128)(2,1)S(1)} %multiply_convert_fusion), channel_id=1, replica_groups=mesh['dp'=8,'cy'=4,'cz'=8] {'cy'}, dimensions={0}, use_global_device_ids=true | all-gather | bytes 655360 | tf_op jit(solution)/shard_map/all_gather | solution.py:49
  300.0 49.8 %all-gather.8.cloned.1.call-done = bf16[512,4096]{1,0:T(8,128)(2,1)} async-done(((bf16[64,4096]{1,0:T(8,128)(2,1)}), bf16[512,4096]{1,0:T(8,128)(2,1)}) %all-gather.8.cloned.1.call-update) | async-done | bytes 4194320 | tf_op jit(solution)/shard_map/all_gather | solution.py:49
  349.8 5.6 %fusion.170 = f32[512,352]{0,1:T(8,128)} fusion(bf16[512,4096]{1,0:T(8,128)(2,1)} %all-gather.8.cloned.1.call-done, bf16[4096,352]{0,1:T(8,128)(2,1)} %param.21), kind=kOutput, calls=%fused_computation.286 | convolution fusion | flops 1476395008 | bytes 7798784 | tf_op jit(solution)/shard_map/dot_general | solution.py:164
  355.4 9.2 %convolution_convert_fusion.1 = bf16[512,4096]{1,0:T(8,128)(2,1)} fusion(bf16[352,4096]{1,0:T(8,128)(2,1)S(1)} %copy-done, bf16[512,4096]{1,0:T(8,128)(2,1)} %all-gather.8.cloned.1.call-done, bf16[4096,352]{0,1:T(8,128)(2,1)} %param.22, f32[512,352]{0,1:T(8,128)} %fusion.170), kind=kOutput, calls=%fused_computation.11 | convolution fusion | flops 2955968512 | bytes 14876672 | tf_op jit(solution)/shard_map/dot_general | solution.py:168
  367.1 53.0 %all_to_all.31 = bf16[8,4,16,4096]{3,2,0,1:T(8,128)(2,1)} all-to-all(bf16[8,4,16,4096]{3,2,0,1:T(8,128)(2,1)S(1)} %copy.39), channel_id=1, replica_groups=mesh['dp'=8,'cy'=4,'cz'=8] {'cy'}, dimensions={1} | all-to-all | bytes 8388608 | tf_op jit(solution)/shard_map/all_to_all | solution.py:42
  424.3 4.3 all-to-all-start.4
  429.0 27.4 %all-to-all-done.4 = bf16[8,16,4096]{2,1,0:T(8,128)(2,1)} async-done(((bf16[8,16,4096]{2,1,0:T(8,128)(2,1)}), bf16[8,16,4096]{2,1,0:T(8,128)(2,1)}, u32[]{:S(2)}, u32[]{:S(2)}) %all-to-all-start.4) | async-done | bytes 1048608 | tf_op jit(solution)/shard_map/all_to_all | solution.py:44
  459.5 5.0 all-to-all-start.5
  466.0 48.7 %all-to-all-done.5 = bf16[32,8,4096]{2,1,0:T(8,128)(2,1)} async-done(((bf16[32,8,4096]{2,1,0:T(8,128)(2,1)}), bf16[32,8,4096]{2,1,0:T(8,128)(2,1)}, u32[]{:S(2)}, u32[]{:S(2)}) %all-to-all-start.5) | async-done | bytes 2097184 | tf_op jit(solution)/shard_map/all_to_all | solution.py:183
  514.8 5.0 gather_fusion.4
  (125 shorter events, 52.9 us)
Async XLA Ops:
  6.5 348.9 %copy-start = (bf16[352,4096]{1,0:T(8,128)(2,1)S(1)}, bf16[352,4096]{1,0:T(8,128)(2,1)}, u32[]{:S(2)}) copy-start(bf16[352,4096]{1,0:T(8,128)(2,1)} %param.23) | copy-start | bytes 8650756
  6.5 36.6 %all-gather.4.cloned.1.call-start = ((), (), s32[]{:S(2)}) async-start(), calls=%async_computation.6 | async-start | bytes 1351680 | tf_op jit(solution)/shard_map/all_gather | solution.py:49
  7.4 2.7 copy-start.4
  13.4 128.8 %all-gather.6.cloned.1.call-start = ((), (), s32[]{:S(2)}) async-start(), calls=%async_computation.7 | async-start | bytes 9732096 | tf_op jit(solution)/shard_map/all_gather | solution.py:49
  144.1 5.2 copy-start.6
  144.1 5.2 copy-start.7
  144.1 5.2 copy-start.8
  155.6 24.1 %all-to-all-start = ((bf16[32,2,4,1024]{3,2,1,0:T(4,128)(2,1)}), bf16[32,2,4,1024]{3,2,1,0:T(4,128)(2,1)}, u32[]{:S(2)}, u32[]{:S(2)}) async-start(bf16[32,2,4,1024]{3,2,1,0:T(4,128)(2,1)} %bitcast.61), calls=%async_computation | async-start | bytes 1048576 | tf_op jit(solution)/shard_map/all_to_all | solution.py:119
  165.4 19.3 %copy-start.3 = (f32[64]{0:T(128)S(1)}, f32[64]{0:T(128)}, u32[]{:S(2)}) copy-start(f32[64]{0:T(128)} %multiply_power_fusion) | copy-start | bytes 772
  186.9 1.9 copy-start.1
  247.9 38.4 %copy-start.2 = (f32[4096]{0:T(1024)S(1)}, f32[4096]{0:T(1024)}, u32[]{:S(2)}) copy-start(f32[4096]{0:T(1024)} %param.20) | copy-start | bytes 49156
  252.1 32.6 %all-to-all-start.2 = ((bf16[8,16,4096]{2,1,0:T(8,128)(2,1)}), bf16[8,16,4096]{2,1,0:T(8,128)(2,1)}, u32[]{:S(2)}, u32[]{:S(2)}) async-start(bf16[8,16,4096]{2,1,0:T(8,128)(2,1)} %reduce_sum.120), calls=%async_computation.2 | async-start | bytes 2097152 | tf_op jit(solution)/shard_map/all_to_all | solution.py:44
  257.8 92.0 %all-gather.8.cloned.1.call-start = ((), (), s32[]{:S(2)}) async-start(), calls=%async_computation.8 | async-start | bytes 4718592 | tf_op jit(solution)/shard_map/all_gather | solution.py:49
  424.3 32.0 %all-to-all-start.4 = ((bf16[8,16,4096]{2,1,0:T(8,128)(2,1)}), bf16[8,16,4096]{2,1,0:T(8,128)(2,1)}, u32[]{:S(2)}, u32[]{:S(2)}) async-start(bf16[8,16,4096]{2,1,0:T(8,128)(2,1)} %reduce_sum.123), calls=%async_computation.4 | async-start | bytes 2097152 | tf_op jit(solution)/shard_map/all_to_all | solution.py:44
  459.5 55.3 %all-to-all-start.5 = ((bf16[32,8,4096]{2,1,0:T(8,128)(2,1)}), bf16[32,8,4096]{2,1,0:T(8,128)(2,1)}, u32[]{:S(2)}, u32[]{:S(2)}) async-start(bf16[32,8,4096]{2,1,0:T(8,128)(2,1)} %select_select_fusion), calls=%async_computation.5 | async-start | bytes 4194304 | tf_op jit(solution)/shard_map/all_to_all | solution.py:183
  514.8 5.0 copy-start.5
Sparse Core Ops, SparseCore 0:
  13.5 29.5 all-gather.3
  44.9 97.1 all-gather.5
  300.1 49.6 all-gather.7
where the time goes:
time: 530 us; the launch traced here: 529 us
  waiting for transfers between devices  256 us (48%)
  blocking collectives  116 us (22%)
  other arithmetic  58.1 us (11%)
  matrix products  34.9 us (7%)
  local copies, waits for them, and re-layouts  27.5 us (5%)
  starting transfers between devices  22.8 us (4%)
  between operations  13.4 us (3%)
    all_gather x2, waiting for transfers between devices, gather_rows(): lax.all_gather(lax.all_gather(x, 'cy', axis=0, tiled=True), 'cz', axis=0,...  122 us
    all_to_all x2, blocking collectives, reduce_scatter_rows(): over_y = lax.all_to_all(blocks, 'cy', 1, 1, tiled=True)  103 us
    all_to_all x1, waiting for transfers between devices, body(): lax.all_to_all(back, GROUP, 0, 0, tiled=True)  48.7 us
    all_to_all x2, waiting for transfers between devices, reduce_scatter_rows(): over_z = lax.all_to_all(part, 'cz', 0, 0, tiled=True)  48.6 us
    all_gather x1, waiting for transfers between devices, gather_rows(): lax.all_gather(x, 'cy', axis=0, tiled=True)  29.7 us
    mul x1, other arithmetic, body(): slot_pos = block_dev[slot_ids // MOST] * tok_local + all_index  15.4 us
    all_gather x1, blocking collectives, gather_rows(): lax.all_gather(x, 'cy', axis=0, tiled=True)  13.5 us
  transfers between devices with their start and end apart: 7, of which 7 were waited for; matrix products, arithmetic and copies ran while one was open for 8% of the time, Pallas kernels for 0%

commit v1 on v0

--- a/solution.py
+++ b/solution.py
@@ -2,6 +2,7 @@
 import jax.numpy as jnp
 from jax import lax
 from jax.sharding import Mesh, PartitionSpec as P
+from jax.lax import all_to_all, axis_size
 
 QUERY_HEADS = 32
 KEY_VALUE_HEADS = 8
@@ -46,7 +47,18 @@
 
 
 def gather_rows(x):
-    return lax.all_gather(lax.all_gather(x, "cy", axis=0, tiled=True), "cz", axis=0, tiled=True)
+
+    def update_wires_on_mesh(message):
+        earlier = all_to_all(
+            jnp.stack(axis_size("cz") * [message], axis=0),
+            axis_name="cz",
+            split_axis=0,
+            concat_axis=0,
+        )
+        tall = jnp.concatenate(earlier, axis=0)
+        return tall
+
+    return update_wires_on_mesh(lax.all_gather(x, "cy", axis=0, tiled=True))
 
 
 def body(

time: 530 us -> 669 us (1.26)
  blocking collectives: 116 us -> 207 us
  waiting for transfers between devices: 256 us -> 293 us
  local copies, waits for them, and re-layouts: 27.5 us -> 34.6 us
    all_to_all x0 -> x1, waiting for transfers between devices: none -> 164 us  [update_wires_on_mesh(): all_to_all(jnp.stack(axis_size('cz') * [message], axis=0), axis_name='cz'...]
    all_gather x3 -> x1, waiting for transfers between devices: 152 us -> 29.8 us  [gather_rows(): return update_wires_on_mesh(lax.all_gather(x, 'cy', axis=0, tiled=True))]
    all_to_all x0 -> x1, blocking collectives: none -> 95.9 us  [update_wires_on_mesh(): all_to_all(jnp.stack(axis_size('cz') * [message], axis=0), axis_name='cz'...]
    all_to_all x0 -> x1, starting transfers between devices: none -> 7.01 us  [update_wires_on_mesh(): all_to_all(jnp.stack(axis_size('cz') * [message], axis=0), axis_name='cz'...]
  transfers between devices with their start and end apart: 7 -> 6, of which waited for: 7 -> 6; matrix products, arithmetic and copies ran while one was open for 8% -> 7% of each run, Pallas kernels for 0% -> 0%
where the time goes in v1:
time: 669 us; the launch traced here: 668 us
  waiting for transfers between devices  293 us (44%)
  blocking collectives  207 us (31%)
  other arithmetic  58.3 us (9%)
  local copies, waits for them, and re-layouts  34.6 us (5%)
  matrix products  33 us (5%)
  starting transfers between devices  27.7 us (4%)
  between operations  13.7 us (2%)
    all_to_all x1, waiting for transfers between devices, update_wires_on_mesh(): all_to_all(jnp.stack(axis_size('cz') * [message], axis=0), axis_name='cz'...  164 us
    all_to_all x2, blocking collectives, reduce_scatter_rows(): over_y = lax.all_to_all(blocks, 'cy', 1, 1, tiled=True)  98 us
    all_to_all x1, blocking collectives, update_wires_on_mesh(): all_to_all(jnp.stack(axis_size('cz') * [message], axis=0), axis_name='cz'...  95.9 us
    all_to_all x2, waiting for transfers between devices, reduce_scatter_rows(): over_z = lax.all_to_all(part, 'cz', 0, 0, tiled=True)  46.4 us
    all_to_all x1, waiting for transfers between devices, body(): lax.all_to_all(back, GROUP, 0, 0, tiled=True)  45.4 us
    all_gather x1, waiting for transfers between devices, gather_rows(): return update_wires_on_mesh(lax.all_gather(x, 'cy', axis=0, tiled=True))  29.8 us
    mul x1, other arithmetic, body(): slot_pos = block_dev[slot_ids // MOST] * tok_local + all_index  15.6 us
  transfers between devices with their start and end apart: 6, of which 6 were waited for; matrix products, arithmetic and copies ran while one was open for 7% of the time, Pallas kernels for 0%

profile of v1, /device:TPU:2, one launch (start us, length us, event | category | flops | bytes accessed | tf_op | source)
XLA Modules:
  0.0 667.7 jit_solution(14712010532372951164)
XLA Ops:
  13.4 29.8 %all-gather.2.cloned.1.call-done = bf16[128,4224]{1,0:T(8,128)(2,1)} async-done(((bf16[32,4224]{1,0:T(8,128)(2,1)}), bf16[128,4224]{1,0:T(8,128)(2,1)}) %all-gather.2.cloned.1.call-update) | async-done | bytes 1081360 | tf_op jit(solution)/shard_map/all_gather | solution.py:61
  43.1 5.6 stack.4
  48.7 7.0 %all-to-all-start = ((bf16[8,128,4224]{2,1,0:T(8,128)(2,1)}), bf16[8,128,4224]{2,1,0:T(8,128)(2,1)}, u32[]{:S(2)}, u32[]{:S(2)}) async-start(bf16[8,128,4224]{2,1,0:T(8,128)(2,1)} %stack.4), calls=%async_computation | async-start | bytes 17301504 | tf_op jit(solution)/shard_map/all_to_all | solution.py:52
  61.2 4.5 select_reduce_fusion
  66.5 15.6 %select_multiply_fusion = s32[1024]{0:T(1024)S(1)} fusion(pred[1024]{0:T(1024)(128)(4,1)S(1)} %fusion.56, pred[1024]{0:T(1024)(128)(4,1)S(1)} %fusion.57, pred[1024]{0:T(1024)(128)(4,1)S(1)} %fusion.80, pred[1024]{0:T(1024)(128)(4,1)S(1)} %fusion.79, pred[1024]{0:T(1024)(128)(4,1)S(1)} %fusion.78, pred[1024]{0:T(1024)(128)(4,1)S(1)} %fusion.77, ...), kind=kLoop, calls=%fused_computation.217 | loop fusion | flops 26624 | bytes 33892 | tf_op jit(solution)/shard_map/mul | solution.py:114
  83.0 164.1 %all-to-all-done = bf16[8,128,4224]{2,1,0:T(8,128)(2,1)} async-done(((bf16[8,128,4224]{2,1,0:T(8,128)(2,1)}), bf16[8,128,4224]{2,1,0:T(8,128)(2,1)}, u32[]{:S(2)}, u32[]{:S(2)}) %all-to-all-start) | async-done | bytes 8650784 | tf_op jit(solution)/shard_map/all_to_all | solution.py:52
  249.1 5.1 fusion
  254.3 6.3 fusion.13
  261.8 4.8 all-to-all-start.1
  268.8 7.2 %fusion.9 = f32[1024,128]{0,1:T(8,128)} fusion(bf16[4096,128]{1,0:T(8,128)(2,1)} %param.16, f32[4096]{0:T(1024)} %param.15, f32[1024]{0:T(1024)S(1)} %add_rsqrt_fusion, bf16[1024,4224]{1,0:T(8,128)(2,1)} %bitcast.3), kind=kOutput, calls=%fused_computation.25 | convolution fusion | flops 1090519040 | bytes 9981952 | tf_op jit(solution)/shard_map/dot_general | solution.py:121
  276.0 7.5 %all-to-all-done.1 = bf16[32,2,4,1024]{3,2,1,0:T(4,128)(2,1)} async-done(((bf16[32,2,4,1024]{3,2,1,0:T(4,128)(2,1)}), bf16[32,2,4,1024]{3,2,1,0:T(4,128)(2,1)}, u32[]{:S(2)}, u32[]{:S(2)}) %all-to-all-start.1) | async-done | bytes 524320 | tf_op jit(solution)/shard_map/all_to_all | solution.py:131
  293.2 5.3 convolution_convert_fusion
  301.0 49.7 %all_to_all.40 = bf16[8,4,16,4096]{3,2,0,1:T(8,128)(2,1)} all-to-all(bf16[8,4,16,4096]{3,2,0,1:T(8,128)(2,1)S(1)} %copy.38), channel_id=1, replica_groups=mesh['dp'=8,'cy'=4,'cz'=8] {'cy'}, dimensions={1} | all-to-all | bytes 8388608 | tf_op jit(solution)/shard_map/all_to_all | solution.py:43
  354.8 6.6 all-to-all-start.3
  361.6 5.3 gather_fusion.2
  366.9 22.2 %all-to-all-done.3 = bf16[8,16,4096]{2,1,0:T(8,128)(2,1)} async-done(((bf16[8,16,4096]{2,1,0:T(8,128)(2,1)}), bf16[8,16,4096]{2,1,0:T(8,128)(2,1)}, u32[]{:S(2)}, u32[]{:S(2)}) %all-to-all-start.3) | async-done | bytes 1048608 | tf_op jit(solution)/shard_map/all_to_all | solution.py:45
  390.8 13.3 %all_gather.7 = bf16[64,4096]{1,0:T(8,128)(2,1)S(1)} all-gather(bf16[16,4096]{1,0:T(8,128)(2,1)S(1)} %multiply_convert_fusion), channel_id=1, replica_groups=mesh['dp'=8,'cy'=4,'cz'=8] {'cy'}, dimensions={0}, use_global_device_ids=true | all-gather | bytes 655360 | tf_op jit(solution)/shard_map/all_gather | solution.py:61
  404.7 95.9 %all_to_all.41 = bf16[8,64,4096]{2,1,0:T(8,128)(2,1)S(1)} all-to-all(bf16[8,64,4096]{2,1,0:T(8,128)(2,1)S(1)} %stack.5), channel_id=1, replica_groups=mesh['dp'=8,'cy'=4,'cz'=8] {'cz'}, dimensions={0} | all-to-all | bytes 8388608 | tf_op jit(solution)/shard_map/all_to_all | solution.py:52
  505.1 9.2 %convolution_convert_fusion.1 = bf16[512,4096]{1,0:T(8,128)(2,1)} fusion(bf16[352,4096]{1,0:T(8,128)(2,1)S(1)} %copy-done, bf16[512,4096]{1,0:T(8,128)(2,1)} %bitcast.63, bf16[4096,352]{0,1:T(8,128)(2,1)} %param.22, f32[512,352]{0,1:T(8,128)} %fusion.170), kind=kOutput, calls=%fused_computation.11 | convolution fusion | flops 2955968512 | bytes 14876672 | tf_op jit(solution)/shard_map/dot_general | solution.py:180
  516.7 48.3 %all_to_all.42 = bf16[8,4,16,4096]{3,2,0,1:T(8,128)(2,1)} all-to-all(bf16[8,4,16,4096]{3,2,0,1:T(8,128)(2,1)S(1)} %copy.39), channel_id=1, replica_groups=mesh['dp'=8,'cy'=4,'cz'=8] {'cy'}, dimensions={1} | all-to-all | bytes 8388608 | tf_op jit(solution)/shard_map/all_to_all | solution.py:43
  573.9 24.1 %all-to-all-done.6 = bf16[8,16,4096]{2,1,0:T(8,128)(2,1)} async-done(((bf16[8,16,4096]{2,1,0:T(8,128)(2,1)}), bf16[8,16,4096]{2,1,0:T(8,128)(2,1)}, u32[]{:S(2)}, u32[]{:S(2)}) %all-to-all-start.6) | async-done | bytes 1048608 | tf_op jit(solution)/shard_map/all_to_all | solution.py:45
  601.2 5.0 all-to-all-start.7
  607.7 45.4 %all-to-all-done.7 = bf16[32,8,4096]{2,1,0:T(8,128)(2,1)} async-done(((bf16[32,8,4096]{2,1,0:T(8,128)(2,1)}), bf16[32,8,4096]{2,1,0:T(8,128)(2,1)}, u32[]{:S(2)}, u32[]{:S(2)}) %all-to-all-start.7) | async-done | bytes 2097184 | tf_op jit(solution)/shard_map/all_to_all | solution.py:195
  653.1 5.0 gather_fusion.4
  (122 shorter events, 60.9 us)
Async XLA Ops:
  6.5 498.5 %copy-start = (bf16[352,4096]{1,0:T(8,128)(2,1)S(1)}, bf16[352,4096]{1,0:T(8,128)(2,1)}, u32[]{:S(2)}) copy-start(bf16[352,4096]{1,0:T(8,128)(2,1)} %param.23) | copy-start | bytes 8650756
  6.5 36.6 %all-gather.2.cloned.1.call-start = ((), (), s32[]{:S(2)}) async-start(), calls=%async_computation.8 | async-start | bytes 1351680 | tf_op jit(solution)/shard_map/all_gather | solution.py:61
  7.4 2.7 copy-start.5
  48.7 198.4 %all-to-all-start = ((bf16[8,128,4224]{2,1,0:T(8,128)(2,1)}), bf16[8,128,4224]{2,1,0:T(8,128)(2,1)}, u32[]{:S(2)}, u32[]{:S(2)}) async-start(bf16[8,128,4224]{2,1,0:T(8,128)(2,1)} %stack.4), calls=%async_computation | async-start | bytes 17301504 | tf_op jit(solution)/shard_map/all_to_all | solution.py:52
  261.8 21.7 %all-to-all-start.1 = ((bf16[32,2,4,1024]{3,2,1,0:T(4,128)(2,1)}), bf16[32,2,4,1024]{3,2,1,0:T(4,128)(2,1)}, u32[]{:S(2)}, u32[]{:S(2)}) async-start(bf16[32,2,4,1024]{3,2,1,0:T(4,128)(2,1)} %bitcast.65), calls=%async_computation.1 | async-start | bytes 1048576 | tf_op jit(solution)/shard_map/all_to_all | solution.py:131
  268.8 18.7 %copy-start.4 = (f32[64]{0:T(128)S(1)}, f32[64]{0:T(128)}, u32[]{:S(2)}) copy-start(f32[64]{0:T(128)} %multiply_power_fusion) | copy-start | bytes 772
  289.7 1.9 copy-start.2
  350.6 40.1 %copy-start.3 = (f32[4096]{0:T(1024)S(1)}, f32[4096]{0:T(1024)}, u32[]{:S(2)}) copy-start(f32[4096]{0:T(1024)} %param.20) | copy-start | bytes 49156
  354.8 34.3 %all-to-all-start.3 = ((bf16[8,16,4096]{2,1,0:T(8,128)(2,1)}), bf16[8,16,4096]{2,1,0:T(8,128)(2,1)}, u32[]{:S(2)}, u32[]{:S(2)}) async-start(bf16[8,16,4096]{2,1,0:T(8,128)(2,1)} %reduce_sum.120), calls=%async_computation.3 | async-start | bytes 2097152 | tf_op jit(solution)/shard_map/all_to_all | solution.py:45
  404.6 97.9 %copy-start.7 = (bf16[4096,352]{0,1:T(8,128)(2,1)S(1)}, bf16[4096,352]{0,1:T(8,128)(2,1)}, u32[]{:S(2)}) copy-start(bf16[4096,352]{0,1:T(8,128)(2,1)} %param.21) | copy-start | bytes 8650756
  500.6 1.9 copy-start.1
  569.3 28.7 %all-to-all-start.6 = ((bf16[8,16,4096]{2,1,0:T(8,128)(2,1)}), bf16[8,16,4096]{2,1,0:T(8,128)(2,1)}, u32[]{:S(2)}, u32[]{:S(2)}) async-start(bf16[8,16,4096]{2,1,0:T(8,128)(2,1)} %reduce_sum.123), calls=%async_computation.6 | async-start | bytes 2097152 | tf_op jit(solution)/shard_map/all_to_all | solution.py:45
  601.2 51.9 %all-to-all-start.7 = ((bf16[32,8,4096]{2,1,0:T(8,128)(2,1)}), bf16[32,8,4096]{2,1,0:T(8,128)(2,1)}, u32[]{:S(2)}, u32[]{:S(2)}) async-start(bf16[32,8,4096]{2,1,0:T(8,128)(2,1)} %select_select_fusion), calls=%async_computation.7 | async-start | bytes 4194304 | tf_op jit(solution)/shard_map/all_to_all | solution.py:195
  653.1 5.0 copy-start.6
Sparse Core Ops, SparseCore 0:
  13.5 29.5 all-gather.1
